TPU v7x, 128 devices: a whole 4x4x4 slice. The times are simulated.
128 devices in a mesh: seq: 32 (over z, x, core), head: 4 (over y).
Axes of the slice: x: 4, y: 4, z: 4, core: 2. Of those that a mesh axis runs over, the one named last changes fastest.
Arguments:
- queries: bfloat16 [16384, 4096], P('seq', 'head'), may hold values from -24 to 24
- key_states: bfloat16 [16384, 4096], P('seq', 'head'), may hold values from -24 to 24
- value_states: bfloat16 [16384, 4096], P('seq', 'head'), may hold values from -6 to 6
- forward_out: bfloat16 [16384, 4096], P('seq', 'head'), may hold values from -3 to 3
- grad_out: bfloat16 [16384, 4096], P('seq', 'head'), may hold values from -96 to 96
- random_blocks: int32 [256, 32, 3], P(None, 'head'), may hold values from 0 to 255, as said below
- global_blocks: int32 [2], replicated, may hold values from 0 to 255, as said below
Outputs:
- grad_queries: bfloat16 [16384, 4096], P(('seq', 'head'))
- grad_keys: bfloat16 [16384, 4096], P(('seq', 'head'))
- grad_values: bfloat16 [16384, 4096], P(('seq', 'head'))
Inputs may be any that keep to these rules, and one draw needn't show every extreme that they name: `random_blocks`: for the query blocks of one shard of 512 tokens and the 8 heads of one head group, at most 8 of the 192 entries name blocks held by any one shard of 8 blocks, and one shard, the same for every group, is named exactly 8 times by every group. `global_blocks`: two different blocks, one of them the last block 255.
All inputs are finite; a program needn't handle non-finite values.
Results may differ from a plain program's by a relative error of at most 0.0053.
Values may be sent and summed in bfloat16 or wider, within the bound.
A program may use at most 128 MiB of HBM per device.

v0:
```python
from functools import partial
import jax
import jax.numpy as jnp
from jax import lax
from jax.sharding import PartitionSpec as P

DH = 128
BS = 64


def padded(cells, sides, width):
    for axis, dim in sides:
        count = lax.axis_size(axis)
        ends = count - 1
        head = lax.slice_in_dim(cells, 0, width, axis=dim)
        tail = lax.slice_in_dim(cells, cells.shape[dim] - width, cells.shape[dim], axis=dim)
        cells = jnp.concatenate(
            [
                lax.ppermute(tail, axis, [(i, (i + 1) % count) for i in range(ends)]),
                cells,
                lax.ppermute(head, axis, [((i + 1) % count, i) for i in range(ends)]),
            ],
            axis=dim,
        )
    return cells


def scaled(values):
    return values * DH ** (-0.5)


def attend(
    query_row_block,
    gradient_row_block,
    saved_rows,
    gathered_key_block,
    gathered_value_block,
    usable,
    outer_max,
    outer_sum,
):
    logit_scores = scaled(
        jnp.einsum(
            "zxp,zufp->zxuf",
            query_row_block,
            gathered_key_block,
            preferred_element_type=jnp.float32,
        )
    )
    logit_scores = jnp.where(usable[:, None, :, None], logit_scores, -jnp.inf)
    peak_score = jnp.maximum(jnp.max(logit_scores, axis=(2, 3)), outer_max)
    row_sum = jnp.sum(jnp.exp(logit_scores - peak_score[:, :, None, None]), axis=(2, 3))
    row_sum = row_sum + outer_sum * jnp.exp(outer_max - peak_score)
    log_norm = peak_score + jnp.log(row_sum)
    weights = jnp.exp(logit_scores - log_norm[:, :, None, None])
    row_dot = jnp.sum(
        gradient_row_block.astype(jnp.float32) * saved_rows.astype(jnp.float32), axis=-1
    )
    weight_gradient = jnp.einsum(
        "zxp,zufp->zxuf",
        gradient_row_block,
        gathered_value_block,
        preferred_element_type=jnp.float32,
    )
    dscores = weights * (weight_gradient - row_dot[:, :, None, None])
    weight_lowp = weights.astype(jnp.bfloat16)
    score_gradient_lowp = dscores.astype(jnp.bfloat16)
    dq_terms = scaled(
        jnp.einsum(
            "bqjk,bjkd->bqjd",
            score_gradient_lowp,
            gathered_key_block,
            preferred_element_type=jnp.float32,
        )
    )
    key_gradient_parts = scaled(
        jnp.einsum(
            "rmnf,rmc->rnfc",
            score_gradient_lowp,
            query_row_block,
            preferred_element_type=jnp.float32,
        )
    )
    value_gradient_parts = jnp.einsum(
        "rmnf,rmc->rnfc", weight_lowp, gradient_row_block, preferred_element_type=jnp.float32
    )
    return (log_norm, row_dot, dq_terms, key_gradient_parts, value_gradient_parts)


def head_pass(operands, usable):
    (
        query_row_block,
        gradient_row_block,
        saved_rows,
        wide_keys,
        wide_values,
        glob_keys,
        glob_values,
        far_keys,
        far_values,
        outer_max,
        outer_sum,
    ) = operands
    block_count = query_row_block.shape[0]

    def listed(wide_rows, glob_rows, far_rows):
        window_set = jnp.stack([wide_rows[:-2], wide_rows[1:-1], wide_rows[2:]], axis=1)
        glob_set = jnp.broadcast_to(glob_rows[None], (block_count,) + glob_rows.shape)
        return jnp.concatenate([window_set, glob_set, far_rows], axis=1)

    log_norm, row_dot, dq_terms, key_gradient_parts, value_gradient_parts = attend(
        query_row_block,
        gradient_row_block,
        saved_rows,
        listed(wide_keys, glob_keys, far_keys),
        listed(wide_values, glob_values, far_values),
        usable,
        outer_max,
        outer_sum,
    )
    far_query = lax.optimization_barrier(dq_terms[:, :, 5:].astype(jnp.bfloat16)).astype(
        jnp.float32
    )
    grad_query = jnp.sum(dq_terms[:, :, :5], axis=2) + jnp.sum(far_query, axis=2)

    def spread(slot_terms):
        widths = ((0, 0), (0, 0), (0, 0))
        first = jnp.pad(slot_terms[:, 0], ((0, 2),) + widths[1:])
        middle = jnp.pad(slot_terms[:, 1], ((1, 1),) + widths[1:])
        last_part = jnp.pad(slot_terms[:, 2], ((2, 0),) + widths[1:])
        return first + middle + last_part

    return (
        grad_query,
        log_norm,
        row_dot,
        spread(key_gradient_parts),
        spread(value_gradient_parts),
        jnp.sum(key_gradient_parts[:, 3:5], axis=0),
        jnp.sum(value_gradient_parts[:, 3:5], axis=0),
        key_gradient_parts[:, 5:].astype(jnp.bfloat16),
        value_gradient_parts[:, 5:].astype(jnp.bfloat16),
    )


def on_device(
    queries, key_states, value_states, forward_out, grad_out, random_blocks, global_blocks
):
    seq_count = lax.axis_size("seq")
    my_seq = lax.axis_index("seq")
    tokens = queries.shape[0]
    blocks = tokens // BS
    head_count = queries.shape[1] // DH
    requests = blocks * head_count * 3
    slot_count = max(2, (5 * requests + 4 * seq_count - 1) // (4 * seq_count))
    kv_pair = jnp.stack([key_states, value_states])
    kv_wide = padded(kv_pair, (("seq", 1),), BS)
    kv_heads = kv_wide.reshape(2, blocks + 2, BS, head_count, DH).transpose(0, 3, 1, 2, 4)
    kv_owned = kv_heads[:, :, 1:-1]
    kv_flat = (
        kv_pair.reshape(2, blocks, BS, head_count, DH)
        .transpose(0, 1, 3, 2, 4)
        .reshape(2, blocks * head_count, BS, DH)
    )
    glob_owner = global_blocks // blocks
    glob_local = global_blocks % blocks
    glob_mine = glob_owner == my_seq
    picked = kv_owned[:, :, glob_local] * glob_mine.astype(jnp.bfloat16)[None, None, :, None, None]
    glob_kv = lax.psum(picked, "seq").astype(jnp.float32).astype(jnp.bfloat16)
    table = random_blocks.reshape(seq_count, requests)
    owner_of = table // blocks
    local_of = table % blocks
    seq_ids = jnp.arange(seq_count, dtype=jnp.int32)
    onehot = (owner_of[:, :, None] == seq_ids[None, None, :]).astype(jnp.int32)
    before = jnp.cumsum(onehot, axis=1) - onehot
    rank_of = jnp.sum(before * onehot, axis=2)
    my_owner = lax.dynamic_index_in_dim(owner_of, my_seq, 0, keepdims=False)
    my_rank = lax.dynamic_index_in_dim(rank_of, my_seq, 0, keepdims=False)
    send_pos = my_owner * slot_count + my_rank
    request_ids = jnp.arange(requests, dtype=jnp.int32)
    pair_of = request_ids // 3
    spill_slot = seq_count * slot_count
    target = jnp.where(
        owner_of == my_seq, seq_ids[:, None] * slot_count + rank_of, spill_slot
    ).reshape(-1)
    head_all = jnp.broadcast_to(pair_of % head_count, (seq_count, requests)).reshape(-1)
    recv_block = (
        jnp.zeros((spill_slot + 1,), jnp.int32).at[target].set(local_of.reshape(-1))[:spill_slot]
    )
    recv_head = jnp.zeros((spill_slot + 1,), jnp.int32).at[target].set(head_all)[:spill_slot]
    recv_used = jnp.zeros((spill_slot + 1,), jnp.float32).at[target].set(1.0)[:spill_slot]
    recv_index = recv_block * head_count + recv_head

    def head_major(array):
        return array.reshape(blocks, BS, head_count, DH).transpose(2, 0, 1, 3)

    query_heads = head_major(queries)
    grad_heads = head_major(grad_out)
    saved_heads = head_major(forward_out)
    block_ids = jnp.arange(blocks)
    always = jnp.ones((blocks,), bool)
    has_prev = (block_ids > 0) | (my_seq > 0)
    has_next = (block_ids < blocks - 1) | (my_seq < seq_count - 1)
    outgoing = kv_flat[:, recv_index]
    incoming = lax.all_to_all(outgoing, "seq", split_axis=1, concat_axis=1, tiled=True)
    fetched = (
        incoming[:, send_pos].reshape(2, blocks, head_count, 3, BS, DH).transpose(0, 2, 1, 3, 4, 5)
    )
    usable = jnp.stack([has_prev, always, has_next, always, always, always, always, always], axis=1)
    outer_max = jnp.full((head_count, blocks, BS), -jnp.inf, jnp.float32)
    outer_sum = jnp.zeros((head_count, blocks, BS), jnp.float32)
    results = lax.map(
        partial(head_pass, usable=usable),
        (
            query_heads,
            grad_heads,
            saved_heads,
            kv_heads[0],
            kv_heads[1],
            glob_kv[0],
            glob_kv[1],
            fetched[0],
            fetched[1],
            outer_max,
            outer_sum,
        ),
    )
    grad_query = results[0]
    far_pack = (
        jnp.stack([results[7], results[8]]).transpose(0, 2, 1, 3, 4, 5).reshape(2, requests, BS, DH)
    )
    sendback = jnp.zeros((2, spill_slot, BS, DH), jnp.bfloat16).at[:, send_pos].set(far_pack)
    returned = lax.all_to_all(sendback, "seq", split_axis=1, concat_axis=1, tiled=True)
    far_grads = returned.astype(jnp.float32) * recv_used[None, :, None, None]
    owned_far = (
        jnp.zeros((2, blocks * head_count, BS, DH), jnp.float32).at[:, recv_index].add(far_grads)
    )
    rim_pack = jnp.stack([results[3], results[4]])
    rim_out = jnp.concatenate([rim_pack[:, :, 0], rim_pack[:, :, -1]], axis=2)
    rim_in = padded(rim_out, (("seq", 2),), BS)
    owned = rim_pack[:, :, 1:-1]
    owned = owned.at[:, :, 0].add(rim_in[:, :, :BS]).at[:, :, -1].add(rim_in[:, :, -BS:])
    glob_sum = lax.psum(jnp.stack([results[5], results[6]]), "seq")
    glob_sum = glob_sum * glob_mine.astype(jnp.float32)[None, None, :, None, None]
    owned = owned.at[:, :, glob_local].add(glob_sum)
    owned = owned + owned_far.reshape(2, blocks, head_count, BS, DH).transpose(0, 2, 1, 3, 4)
    grads_kv = (
        owned.astype(jnp.bfloat16).transpose(0, 2, 3, 1, 4).reshape(2, tokens, head_count * DH)
    )
    dq_rows = grad_query.astype(jnp.bfloat16).transpose(1, 2, 0, 3).reshape(tokens, head_count * DH)
    out_query, out_keys, out_values = (
        lax.all_to_all(dq_rows, "head", split_axis=0, concat_axis=1, tiled=True),
        lax.all_to_all(grads_kv[0], "head", split_axis=0, concat_axis=1, tiled=True),
        lax.all_to_all(grads_kv[1], "head", split_axis=0, concat_axis=1, tiled=True),
    )
    return (out_query, out_keys, out_values)


def solution(mesh):
    return jax.shard_map(
        on_device,
        mesh=mesh,
        in_specs=(
            P("seq", "head"),
            P("seq", "head"),
            P("seq", "head"),
            P("seq", "head"),
            P("seq", "head"),
            P(None, "head", None),
            P(),
        ),
        out_specs=(P(("seq", "head"), None), P(("seq", "head"), None), P(("seq", "head"), None)),
        check_vma=False,
    )
```

profile of v0, /device:TPU:2, one launch (start us, length us, event | category | flops | bytes accessed | tf_op | source)
XLA Modules:
  0.0 855.4 jit_solution(16249413253305519232)
XLA Ops:
  10.5 18.4 %reduce-window.6 = s32[32,32,2,128]{3,1,2,0:T(8,128)S(1)} reduce-window(s32[32,32,2,128]{3,1,2,0:T(8,128)S(1)} %copy_bitcast_fusion.1, s32[]{:T(128)} %constant.212.clone.1), window={size=1x1x1x128 pad=0_0x0_0x0_0x127_0}, to_apply=%region_1.2 | reduce-window | flops 33292288 | bytes 2097156 | tf_op jit(solution)/shard_map/reduce-window
  31.0 23.0 %scatter_custom_fusion = s32[257]{0:T(512)S(1)} fusion(s32[6144]{0:T(1024)S(1)} %bitcast.346, s32[6144]{0:T(1024)S(1)} %add_select_fusion.1, s32[]{:T(128)} %constant.212.clone.1), kind=kCustom, calls=%fused_computation.170 | custom fusion | bytes 1032 | tf_op jit(solution)/shard_map/scatter | solution.py:188
  54.0 23.0 %scatter_custom_fusion.1 = s32[257]{0:T(512)S(1)} fusion(s32[6144]{0:T(1024)S(1)} %bitcast.347, s32[6144]{0:T(1024)S(1)} %reshape.454, s32[]{:T(128)} %constant.212.clone.1), kind=kCustom, calls=%fused_computation.168 | custom fusion | bytes 1032 | tf_op jit(solution)/shard_map/scatter | solution.py:190
  78.3 8.6 %gather_fusion.1 = bf16[256,2,64,128]{3,2,1,0:T(8,128)(2,1)} fusion(bf16[2,64,64,128]{3,2,1,0:T(8,128)(2,1)S(1)} %bitcast.306, s32[1024]{0:T(1024)S(1)} %pad_clamp_fusion.1), kind=kCustom, calls=%fused_computation.1 | custom fusion | bytes 16778240 | tf_op jit(solution)/shard_map/gather | solution.py:204
  87.0 8.6 %all-to-all-start = ((bf16[2,256,64,128]{3,2,0,1:T(8,128)(2,1)}), bf16[2,256,64,128]{3,2,0,1:T(8,128)(2,1)}, u32[]{:S(2)}, u32[]{:S(2)}) async-start(bf16[2,256,64,128]{3,2,0,1:T(8,128)(2,1)} %bitcast.307), calls=%async_computation | async-start | bytes 16777216 | tf_op jit(solution)/shard_map/all_to_all | solution.py:205
  98.6 3.5 collective-permute-start.1
  113.2 2.5 copy.130
  117.1 76.9 %collective-permute-done = bf16[2,64,1024]{2,1,0:T(8,128)(2,1)S(1)} collective-permute-done((bf16[2,64,1024]{2,1,0:T(8,128)(2,1)}, bf16[2,64,1024]{2,1,0:T(8,128)(2,1)S(1)}, u32[]{:S(2)}, u32[]{:S(2)}) %collective-permute-start) | collective-permute-done | bytes 262176 | tf_op jit(solution)/shard_map/ppermute | solution.py:19
  206.1 107.6 %all-reduce.10.cloned.1.call-done = bf16[2,8,2,64,128]{4,3,1,0,2:T(8,128)(2,1)} async-done(((bf16[2,8,2,64,128]{4,3,1,0,2:T(8,128)(2,1)}), bf16[2,8,2,64,128]{4,3,1,0,2:T(8,128)(2,1)}) %all-reduce.10.cloned.1.call-update) | async-done | bytes 524304 | tf_op jit(solution)/shard_map/psum | solution.py:169
  314.7 11.5 %gather_fusion.2 = bf16[192,2,64,128]{3,2,1,0:T(8,128)(2,1)} fusion(bf16[2,256,64,128]{3,2,0,1:T(8,128)(2,1)} %all-to-all-done, s32[1024]{0:T(1024)S(1)} %pad_clamp_fusion), kind=kCustom, calls=%fused_computation.2 | custom fusion | bytes 12583680 | tf_op jit(solution)/shard_map/gather | solution.py:207
  326.2 4.3 copy.126
  330.5 4.1 slice_bitcast_fusion.6
  334.7 149.4 %while.26 = (s32[]{:T(128)}, bf16[8,8,64,128]{3,2,1,0:T(8,128)(2,1)S(1)}, f32[8,10,64,128]{3,2,0,1:T(8,128)}, f32[8,10,64,128]{3,2,0,1:T(8,128)}, f32[8,2,64,128...) while((s32[]{:T(128)}, ...), condition=%wide.region_14.15_spmd, body=%wide.region_6.14_spmd.sunk | while | flops 340951552 | bytes 32071516 | solution.py:212
  484.1 3.8 pad_maximum_fusion
  487.9 4.1 copy.142
  492.0 5.5 broadcast_in_dim.140
  497.5 29.1 %scatter_fusion = bf16[2,256,64,128]{3,2,1,0:T(8,128)(2,1)} fusion(bf16[2,256,64,128]{3,2,1,0:T(8,128)(2,1)} %broadcast_in_dim.140, s32[192]{0:T(256)S(1)} %bitcast.350, bf16[192,2,64,128]{3,2,1,0:T(8,128)(2,1)} %copy.142), kind=kCustom, calls=%fused_computation.5 | custom fusion | bytes 18875136 | tf_op jit(solution)/shard_map/scatter | solution.py:232
  526.5 9.7 %copy.143 = bf16[2,256,64,128]{3,2,0,1:T(8,128)(2,1)} copy(bf16[2,256,64,128]{3,2,1,0:T(8,128)(2,1)} %scatter_fusion) | data formatting | bytes 16777216 | tf_op jit(solution)/shard_map/scatter | solution.py:232
  536.2 6.7 all-to-all-start.2
  550.2 96.7 %collective-permute-done.2 = f32[2,8,64,128]{3,2,1,0:T(8,128)} collective-permute-done((f32[2,8,64,128]{3,2,1,0:T(8,128)}, f32[2,8,64,128]{3,2,1,0:T(8,128)}, u32[]{:S(2)}, u32[]{:S(2)}) %collective-permute-start.2) | collective-permute-done | bytes 524320 | tf_op jit(solution)/shard_map/ppermute | solution.py:19
  652.0 23.0 %scatter_custom_fusion.3 = f32[257]{0:T(512)S(1)} fusion(s32[6144]{0:T(1024)S(1)} %bitcast.348, f32[6144]{0:T(1024)S(1)} %broadcast.368, f32[]{:T(128)} %constant.213.clone.1), kind=kCustom, calls=%fused_computation.166 | custom fusion | bytes 1032 | tf_op jit(solution)/shard_map/scatter | solution.py:191
  678.2 40.5 %all-reduce.12.cloned.1.call-done = f32[2,8,2,64,128]{4,3,2,1,0:T(8,128)} async-done(((f32[2,8,2,64,128]{4,3,2,1,0:T(8,128)}), f32[2,8,2,64,128]{4,3,2,1,0:T(8,128)}) %all-reduce.12.cloned.1.call-update) | async-done | bytes 1048592 | tf_op jit(solution)/shard_map/psum | solution.py:243
  724.3 4.5 all-to-all-start.1
  728.8 10.4 %multiply_bitcast_fusion.1 = f32[256,2,64,128]{3,2,1,0:T(8,128)} fusion(bf16[2,256,64,128]{3,2,0,1:T(8,128)(2,1)} %all-to-all-done.2, f32[256]{0:T(256)S(1)} %slice-done), kind=kLoop, calls=%fused_computation.73 | loop fusion | flops 8388608 | bytes 25166848 | tf_op jit(solution)/shard_map/mul | solution.py:234
  741.7 51.7 %scatter_fusion.1 = f32[2,64,64,128]{3,2,1,0:T(8,128)} fusion(f32[2,64,64,128]{3,2,1,0:T(8,128)} %broadcast_in_dim.139, s32[256]{0:T(256)S(1)} %compare_select_fusion.6, f32[256,2,64,128]{3,2,1,0:T(8,128)} %multiply_bitcast_fusion.1), kind=kCustom, calls=%fused_computation.7 | custom fusion | flops 4194304 | bytes 50332672 | tf_op jit(solution)/shard_map/scatter-add | solution.py:236
  793.4 6.8 bitcast_add_fusion
  800.1 3.1 scatter_fusion.2
  803.2 2.7 convert_bitcast_fusion
  809.1 4.7 all-to-all-start.3
  817.0 11.7 %all-to-all-done.3 = bf16[4,128,1024]{2,1,0:T(8,128)(2,1)S(1)} async-done(((bf16[4,128,1024]{2,1,0:T(8,128)(2,1)}), bf16[4,128,1024]{2,1,0:T(8,128)(2,1)S(1)}, u32[]{:S(2)}, u32[]{:S(2)}) %all-to-all-start.3) | async-done | bytes 1048608 | tf_op jit(solution)/shard_map/all_to_all | solution.py:253
  828.7 3.5 all-to-all-start.4
  837.8 8.5 all-to-all-done.4
  (381 shorter events, 220.3 us)
Async XLA Ops:
  29.0 48.0 %copy-start.5 = (bf16[512,1024]{1,0:T(8,128)(2,1)S(1)}, bf16[512,1024]{1,0:T(8,128)(2,1)}, u32[]{:S(2)}) copy-start(bf16[512,1024]{1,0:T(8,128)(2,1)} %param.14) | copy-start | bytes 3145732
  29.8 47.5 %copy-start.4 = (bf16[512,1024]{1,0:T(8,128)(2,1)S(1)}, bf16[512,1024]{1,0:T(8,128)(2,1)}, u32[]{:S(2)}) copy-start(bf16[512,1024]{1,0:T(8,128)(2,1)} %param.15) | copy-start | bytes 3145732
  87.0 8.7 %copy-start.6 = (bf16[512,1024]{1,0:T(8,128)(2,1)S(1)}, bf16[512,1024]{1,0:T(8,128)(2,1)}, u32[]{:S(2)}) copy-start(bf16[512,1024]{1,0:T(8,128)(2,1)} %param.14) | copy-start | bytes 3145732
  87.0 227.7 %all-to-all-start = ((bf16[2,256,64,128]{3,2,0,1:T(8,128)(2,1)}), bf16[2,256,64,128]{3,2,0,1:T(8,128)(2,1)}, u32[]{:S(2)}, u32[]{:S(2)}) async-start(bf16[2,256,64,128]{3,2,0,1:T(8,128)(2,1)} %bitcast.307), calls=%async_computation | async-start | bytes 16777216 | tf_op jit(solution)/shard_map/all_to_all | solution.py:205
  95.6 6.5 copy-start.9
  95.6 218.0 %all-reduce.10.cloned.1.call-start = ((), (), s32[]{:S(2)}) async-start(), calls=%async_computation.5 | async-start | bytes 1048576 | tf_op jit(solution)/shard_map/psum | solution.py:169
  96.6 97.4 %collective-permute-start = (bf16[2,64,1024]{2,1,0:T(8,128)(2,1)}, bf16[2,64,1024]{2,1,0:T(8,128)(2,1)S(1)}, u32[]{:S(2)}, u32[]{:S(2)}) collective-permute-start(bf16[2,64,1024]{2,1,0:T(8,128)(2,1)} %get-tuple-element.381), channel_id=1, source_target_pairs={{0,4},{4,8},{8,12},{12,16},{16,20},{20,24},{24,28},{28,32},{32,36}... | collective-permute-start | bytes 786440 | tf_op jit(solution)/shard_map/ppermute | solution.py:19
  98.6 97.4 %collective-permute-start.1 = (bf16[2,64,1024]{2,1,0:T(8,128)(2,1)}, bf16[2,64,1024]{2,1,0:T(8,128)(2,1)}, u32[]{:S(2)}, u32[]{:S(2)}) collective-permute-start(bf16[2,64,1024]{2,1,0:T(8,128)(2,1)} %get-tuple-element.382), channel_id=1, source_target_pairs={{4,0},{8,4},{12,8},{16,12},{20,16},{24,20},{28,24},{32,28},{36,32}... | collective-permute-start | bytes 786440 | tf_op jit(solution)/shard_map/ppermute | solution.py:21
  102.1 3.8 copy-start.10
  102.2 5.0 copy-start.16
  107.2 3.7 copy-start.8
  112.0 3.8 copy-start.7
  330.5 4.2 copy-start.11
  330.5 4.2 copy-start.13
  484.1 3.8 copy-start.12
  536.2 6.8 copy-start
  536.2 188.1 %all-to-all-start.2 = ((bf16[2,256,64,128]{3,2,0,1:T(8,128)(2,1)}), bf16[2,256,64,128]{3,2,0,1:T(8,128)(2,1)}, u32[]{:S(2)}, u32[]{:S(2)}) async-start(bf16[2,256,64,128]{3,2,0,1:T(8,128)(2,1)} %copy.143), calls=%async_computation.2 | async-start | bytes 16777216 | tf_op jit(solution)/shard_map/all_to_all | solution.py:233
  543.0 175.7 %all-reduce.12.cloned.1.call-start = ((), (), s32[]{:S(2)}) async-start(), calls=%async_computation.6 | async-start | bytes 2097152 | tf_op jit(solution)/shard_map/psum | solution.py:243
  543.0 3.9 copy-start.14
  544.9 102.0 %collective-permute-start.2 = (f32[2,8,64,128]{3,2,1,0:T(8,128)}, f32[2,8,64,128]{3,2,1,0:T(8,128)}, u32[]{:S(2)}, u32[]{:S(2)}) collective-permute-start(f32[2,8,64,128]{3,2,1,0:T(8,128)} %fusion.31), channel_id=1, source_target_pairs={{0,4},{4,8},{8,12},{12,16},{16,20},{20,24},{24,28},{28,32},{32,36}... | collective-permute-start | bytes 1572872 | tf_op jit(solution)/shard_map/ppermute | solution.py:19
  548.0 98.9 %copy-start.1 = (f32[8,10,64,128]{3,2,0,1:T(8,128)S(1)}, f32[8,10,64,128]{3,2,0,1:T(8,128)}, u32[]{:S(2)}) copy-start(f32[8,10,64,128]{3,2,0,1:T(8,128)} %get-tuple-element.255) | copy-start | bytes 7864324
  648.0 2.0 copy-start.2
  650.1 73.4 %collective-permute-start.3 = (f32[2,8,64,128]{3,2,1,0:T(8,128)S(1)}, f32[2,8,64,128]{3,2,1,0:T(8,128)S(1)}, u32[]{:S(2)}, u32[]{:S(2)}) collective-permute-start(f32[2,8,64,128]{3,2,1,0:T(8,128)S(1)} %get-tuple-element.375), channel_id=1, source_target_pairs={{4,0},{8,4},{12,8},{16,12},{20,16},{24,20},{28,24},{32,28},{36,32}... | collective-permute-start | bytes 1572872 | tf_op jit(solution)/shard_map/ppermute | solution.py:21
  675.0 45.3 %copy-start.15 = (f32[257]{0:T(512)}, f32[257]{0:T(512)S(1)}, u32[]{:S(2)}) copy-start(f32[257]{0:T(512)S(1)} %scatter_custom_fusion.3) | copy-start | bytes 3088
  718.7 2.5 copy-start.3
  723.4 5.4 slice-start
  724.3 84.8 %all-to-all-start.1 = ((bf16[4,128,1024]{2,1,0:T(8,128)(2,1)}), bf16[4,128,1024]{2,1,0:T(8,128)(2,1)S(1)}, u32[]{:S(2)}, u32[]{:S(2)}) async-start(bf16[4,128,1024]{2,1,0:T(8,128)(2,1)} %all_to_all.49), calls=%async_computation.1 | async-start | bytes 2097152 | tf_op jit(solution)/shard_map/all_to_all | solution.py:252
  809.1 19.7 %all-to-all-start.3 = ((bf16[4,128,1024]{2,1,0:T(8,128)(2,1)}), bf16[4,128,1024]{2,1,0:T(8,128)(2,1)S(1)}, u32[]{:S(2)}, u32[]{:S(2)}) async-start(bf16[4,128,1024]{2,1,0:T(8,128)(2,1)} %all_to_all.54), calls=%async_computation.3 | async-start | bytes 2097152 | tf_op jit(solution)/shard_map/all_to_all | solution.py:253
  828.7 17.6 %all-to-all-start.4 = ((bf16[4,128,1024]{2,1,0:T(8,128)(2,1)}), bf16[4,128,1024]{2,1,0:T(8,128)(2,1)S(1)}, u32[]{:S(2)}, u32[]{:S(2)}) async-start(bf16[4,128,1024]{2,1,0:T(8,128)(2,1)} %all_to_all.58), calls=%async_computation.4 | async-start | bytes 2097152 | tf_op jit(solution)/shard_map/all_to_all | solution.py:254
Sparse Core Ops, SparseCore 0:
  203.9 109.7 all-reduce.9
  548.1 170.5 all-reduce.11
where the time goes:
time: 868 us; the launch traced here: 855 us
  waiting for transfers between devices  344 us (40%)
  local copies, waits for them, and re-layouts  277 us (32%)
  other arithmetic  132 us (15%)
  matrix products  47.9 us (6%)
  starting transfers between devices  37.7 us (4%)
  between operations  14.9 us (2%)
    ppermute x2, waiting for transfers between devices, padded(): lax.ppermute(tail, axis, [(i, (i + 1) % count) for i in range(ends)])  174 us
    psum x1, waiting for transfers between devices, on_device(): glob_kv = lax.psum(picked, 'seq').astype(jnp.float32).astype(jnp.bfloat16)  108 us
    scatter-add x1, other arithmetic, on_device(): jnp.zeros((2, blocks * head_count, BS, DH), jnp.float32).at[:, recv_index]  51.7 us
    while x64, local copies, waits for them, and re-layouts  45.7 us
    psum x1, waiting for transfers between devices, on_device(): glob_sum = lax.psum(jnp.stack([results[5], results[6]]), 'seq')  40.5 us
    scatter x2, local copies, waits for them, and re-layouts, on_device(): jnp.zeros((2, spill_slot, BS, DH), jnp.bfloat16).at[:, send_pos]  38.8 us
    another operation x11, other arithmetic  25.8 us
    scatter x1, local copies, waits for them, and re-layouts, on_device(): jnp.zeros((spill_slot + 1,), jnp.int32).at[target].set(head_all)  23 us
  transfers between devices with their start and end apart: 11, of which 7 were waited for; matrix products, arithmetic and copies ran while one was open for 17% of the time, Pallas kernels for 0%

commit v1 on v0

--- a/solution.py
+++ b/solution.py
@@ -166,7 +166,11 @@
     glob_local = global_blocks % blocks
     glob_mine = glob_owner == my_seq
     picked = kv_owned[:, :, glob_local] * glob_mine.astype(jnp.bfloat16)[None, None, :, None, None]
-    glob_kv = lax.psum(picked, "seq").astype(jnp.float32).astype(jnp.bfloat16)
+
+    def _connect_tasks(tile_in):
+        return lax.all_gather(tile_in, "seq").sum(axis=0)
+
+    glob_kv = _connect_tasks(picked).astype(jnp.float32).astype(jnp.bfloat16)
     table = random_blocks.reshape(seq_count, requests)
     owner_of = table // blocks
     local_of = table % blocks

time: 868 us -> 794 us (0.915)
  waiting for transfers between devices: 344 us -> 251 us
  other arithmetic: 132 us -> 156 us
  local copies, waits for them, and re-layouts: 277 us -> 261 us
    psum x1 -> x0, waiting for transfers between devices: 108 us -> none  [on_device(): glob_kv = lax.psum(picked, 'seq').astype(jnp.float32).astype(jnp.bfloat16)]
    all_to_all x1, waiting for transfers between devices: 0.01 us -> 91.9 us  [on_device(): lax.all_to_all(outgoing, 'seq', split_axis=1, concat_axis=1, tiled=True)]
    ppermute x2, waiting for transfers between devices: 174 us -> 97.6 us  [padded(): lax.ppermute(tail, axis, [(i, (i + 1) % count) for i in range(ends)])]
    while x64, local copies, waits for them, and re-layouts: 45.7 us -> 24 us
    another operation x11, other arithmetic: 25.8 us -> 40.6 us
    broadcast_in_dim x16, local copies, waits for them, and re-layouts: 0.19 us -> 12.3 us  [listed(): jnp.broadcast_to(glob_rows[None], (block_count,) + glob_rows.shape)]
    reduce_sum x0 -> x1, other arithmetic: none -> 9.15 us  [_connect_tasks(): return lax.all_gather(tile_in, 'seq').sum(axis=0)]
  transfers between devices with their start and end apart: 11 -> 11, of which waited for: 7 -> 7; matrix products, arithmetic and copies ran while one was open for 17% -> 32% of each run, Pallas kernels for 0% -> 0%
where the time goes in v1:
time: 794 us; the launch traced here: 779 us
  local copies, waits for them, and re-layouts  261 us (33%)
  waiting for transfers between devices  251 us (32%)
  other arithmetic  156 us (20%)
  matrix products  47.9 us (6%)
  starting transfers between devices  46.2 us (6%)
  between operations  14.9 us (2%)
    ppermute x2, waiting for transfers between devices, padded(): lax.ppermute(tail, axis, [(i, (i + 1) % count) for i in range(ends)])  97.6 us
    all_to_all x1, waiting for transfers between devices, on_device(): lax.all_to_all(outgoing, 'seq', split_axis=1, concat_axis=1, tiled=True)  91.9 us
    scatter-add x1, other arithmetic, on_device(): jnp.zeros((2, blocks * head_count, BS, DH), jnp.float32).at[:, recv_index]  51.8 us
    another operation x11, other arithmetic  40.6 us
    psum x1, waiting for transfers between devices, on_device(): glob_sum = lax.psum(jnp.stack([results[5], results[6]]), 'seq')  40.5 us
    scatter x2, local copies, waits for them, and re-layouts, on_device(): jnp.zeros((2, spill_slot, BS, DH), jnp.bfloat16).at[:, send_pos]  38.7 us
    while x64, local copies, waits for them, and re-layouts  24 us
    scatter x1, local copies, waits for them, and re-layouts, on_device(): jnp.zeros((spill_slot + 1,), jnp.float32).at[target].set(1.0)[:spill_slot]  23.2 us
  transfers between devices with their start and end apart: 11, of which 7 were waited for; matrix products, arithmetic and copies ran while one was open for 32% of the time, Pallas kernels for 0%

profile of v1, /device:TPU:2, one launch (start us, length us, event | category | flops | bytes accessed | tf_op | source)
XLA Modules:
  0.0 778.6 jit_solution(12713466689635118469)
XLA Ops:
  10.4 3.6 collective-permute-start.1
  28.9 32.3 %reduce-window.6 = s32[32,32,2,128]{3,1,2,0:T(8,128)S(1)} reduce-window(s32[32,32,2,128]{3,1,2,0:T(8,128)} %copy_bitcast_fusion, s32[]{:T(128)} %constant.214.clone.1), window={size=1x1x1x128 pad=0_0x0_0x0_0x127_0}, to_apply=%region_1.2 | reduce-window | flops 33292288 | bytes 2097156 | tf_op jit(solution)/shard_map/reduce-window
  65.4 23.0 %scatter_custom_fusion = s32[257]{0:T(512)S(1)} fusion(s32[6144]{0:T(1024)S(1)} %bitcast.344, s32[6144]{0:T(1024)S(1)} %add_select_fusion.1, s32[]{:T(128)} %constant.214.clone.1), kind=kCustom, calls=%fused_computation.169 | custom fusion | bytes 1032 | tf_op jit(solution)/shard_map/scatter | solution.py:192
  88.4 23.0 %scatter_custom_fusion.1 = s32[257]{0:T(512)S(1)} fusion(s32[6144]{0:T(1024)S(1)} %bitcast.345, s32[6144]{0:T(1024)S(1)} %reshape.461, s32[]{:T(128)} %constant.214.clone.1), kind=kCustom, calls=%fused_computation.167 | custom fusion | bytes 1032 | tf_op jit(solution)/shard_map/scatter | solution.py:194
  112.7 8.6 %gather_fusion.1 = bf16[256,2,64,128]{3,2,1,0:T(8,128)(2,1)} fusion(bf16[2,64,64,128]{3,2,1,0:T(8,128)(2,1)S(1)} %bitcast.305, s32[1024]{0:T(1024)S(1)} %pad_clamp_fusion.1), kind=kCustom, calls=%fused_computation.1 | custom fusion | bytes 16778240 | tf_op jit(solution)/shard_map/gather | solution.py:208
  121.3 12.4 %all-to-all-start = ((bf16[2,256,64,128]{3,2,0,1:T(8,128)(2,1)}), bf16[2,256,64,128]{3,2,0,1:T(8,128)(2,1)}, u32[]{:S(2)}, u32[]{:S(2)}) async-start(bf16[2,256,64,128]{3,2,0,1:T(8,128)(2,1)} %bitcast.306), calls=%async_computation | async-start | bytes 16777216 | tf_op jit(solution)/shard_map/all_to_all | solution.py:209
  141.1 91.9 %all-to-all-done = bf16[2,256,64,128]{3,2,0,1:T(8,128)(2,1)} async-done(((bf16[2,256,64,128]{3,2,0,1:T(8,128)(2,1)}), bf16[2,256,64,128]{3,2,0,1:T(8,128)(2,1)}, u32[]{:S(2)}, u32[]{:S(2)}) %all-to-all-start) | async-done | bytes 8388640 | tf_op jit(solution)/shard_map/all_to_all | solution.py:209
  233.0 11.5 %gather_fusion.2 = bf16[192,2,64,128]{3,2,1,0:T(8,128)(2,1)} fusion(bf16[2,256,64,128]{3,2,0,1:T(8,128)(2,1)} %all-to-all-done, s32[1024]{0:T(1024)S(1)} %pad_clamp_fusion), kind=kCustom, calls=%fused_computation.2 | custom fusion | bytes 12583680 | tf_op jit(solution)/shard_map/gather | solution.py:211
  244.5 4.3 copy.125
  248.8 4.2 slice_bitcast_fusion.6
  253.0 9.2 %reduce_sum.93 = bf16[2,8,2,64,128]{4,3,2,1,0:T(8,128)(2,1)S(1)} reduce(bf16[32,2,8,2,64,128]{5,4,3,2,1,0:T(8,128)(2,1)} %all-gather.2.cloned.1.call-done, bf16[]{:T(256)} %constant.216.clone.1), dimensions={0}, to_apply=%region_0.1 | reduce | flops 8126464 | bytes 17301506 | tf_op jit(solution)/shard_map/reduce_sum | solution.py:171
  263.0 139.8 %while.26 = (s32[]{:T(128)}, bf16[8,8,64,128]{3,2,1,0:T(8,128)(2,1)S(1)}, f32[8,10,64,128]{3,2,0,1:T(8,128)}, f32[8,10,64,128]{3,2,0,1:T(8,128)}, f32[8,2,64,128...) while((s32[]{:T(128)}, ...), condition=%wide.region_14.15_spmd, body=%wide.region_6.14_spmd.sunk | while | flops 340951552 | bytes 32071516 | solution.py:216
  402.8 3.8 pad_maximum_fusion
  406.6 4.2 copy.143
  410.8 5.4 broadcast_in_dim.140
  416.2 29.1 %scatter_fusion = bf16[2,256,64,128]{3,2,1,0:T(8,128)(2,1)} fusion(bf16[2,256,64,128]{3,2,1,0:T(8,128)(2,1)} %broadcast_in_dim.140, s32[192]{0:T(256)S(1)} %bitcast.348, bf16[192,2,64,128]{3,2,1,0:T(8,128)(2,1)} %copy.143), kind=kCustom, calls=%fused_computation.5 | custom fusion | bytes 18875136 | tf_op jit(solution)/shard_map/scatter | solution.py:236
  445.2 9.6 %copy.144 = bf16[2,256,64,128]{3,2,0,1:T(8,128)(2,1)} copy(bf16[2,256,64,128]{3,2,1,0:T(8,128)(2,1)} %scatter_fusion) | data formatting | bytes 16777216 | tf_op jit(solution)/shard_map/scatter | solution.py:236
  454.9 11.4 %all-to-all-start.2 = ((bf16[2,256,64,128]{3,2,0,1:T(8,128)(2,1)}), bf16[2,256,64,128]{3,2,0,1:T(8,128)(2,1)}, u32[]{:S(2)}, u32[]{:S(2)}) async-start(bf16[2,256,64,128]{3,2,0,1:T(8,128)(2,1)} %copy.144), calls=%async_computation.2 | async-start | bytes 16777216 | tf_op jit(solution)/shard_map/all_to_all | solution.py:237
  473.6 96.9 %collective-permute-done.2 = f32[2,8,64,128]{3,2,1,0:T(8,128)} collective-permute-done((f32[2,8,64,128]{3,2,1,0:T(8,128)}, f32[2,8,64,128]{3,2,1,0:T(8,128)}, u32[]{:S(2)}, u32[]{:S(2)}) %collective-permute-start.2) | collective-permute-done | bytes 524320 | tf_op jit(solution)/shard_map/ppermute | solution.py:19
  575.5 23.2 %scatter_custom_fusion.3 = f32[257]{0:T(512)S(1)} fusion(s32[6144]{0:T(1024)S(1)} %bitcast.346, f32[6144]{0:T(1024)S(1)} %broadcast.375, f32[]{:T(128)} %constant.215.clone.1), kind=kCustom, calls=%fused_computation.165 | custom fusion | bytes 1032 | tf_op jit(solution)/shard_map/scatter | solution.py:195
  601.9 40.5 %all-reduce.9.cloned.1.call-done = f32[2,8,2,64,128]{4,3,2,1,0:T(8,128)} async-done(((f32[2,8,2,64,128]{4,3,2,1,0:T(8,128)}), f32[2,8,2,64,128]{4,3,2,1,0:T(8,128)}) %all-reduce.9.cloned.1.call-update) | async-done | bytes 1048592 | tf_op jit(solution)/shard_map/psum | solution.py:247
  648.1 4.3 all-to-all-start.1
  652.4 10.3 %multiply_bitcast_fusion.1 = f32[256,2,64,128]{3,2,1,0:T(8,128)} fusion(bf16[2,256,64,128]{3,2,0,1:T(8,128)(2,1)} %all-to-all-done.2, f32[256]{0:T(256)S(1)} %slice-done), kind=kLoop, calls=%fused_computation.73 | loop fusion | flops 8388608 | bytes 25166848 | tf_op jit(solution)/shard_map/mul | solution.py:238
  662.6 2.5 broadcast_in_dim.139
  665.1 51.8 %scatter_fusion.1 = f32[2,64,64,128]{3,2,1,0:T(8,128)} fusion(f32[2,64,64,128]{3,2,1,0:T(8,128)} %broadcast_in_dim.139, s32[256]{0:T(256)S(1)} %compare_select_fusion.6, f32[256,2,64,128]{3,2,1,0:T(8,128)} %multiply_bitcast_fusion.1), kind=kCustom, calls=%fused_computation.7 | custom fusion | flops 4194304 | bytes 50332672 | tf_op jit(solution)/shard_map/scatter-add | solution.py:240
  716.9 6.8 bitcast_add_fusion
  723.7 3.1 scatter_fusion.2
  726.8 2.7 convert_bitcast_fusion
  732.7 5.0 all-to-all-start.3
  740.9 11.4 %all-to-all-done.3 = bf16[4,128,1024]{2,1,0:T(8,128)(2,1)S(1)} async-done(((bf16[4,128,1024]{2,1,0:T(8,128)(2,1)}), bf16[4,128,1024]{2,1,0:T(8,128)(2,1)S(1)}, u32[]{:S(2)}, u32[]{:S(2)}) %all-to-all-start.3) | async-done | bytes 1048608 | tf_op jit(solution)/shard_map/all_to_all | solution.py:257
  752.3 3.5 all-to-all-start.4
  761.4 8.2 %all-to-all-done.4 = bf16[4,128,1024]{2,1,0:T(8,128)(2,1)S(1)} async-done(((bf16[4,128,1024]{2,1,0:T(8,128)(2,1)}), bf16[4,128,1024]{2,1,0:T(8,128)(2,1)S(1)}, u32[]{:S(2)}, u32[]{:S(2)}) %all-to-all-start.4) | async-done | bytes 1048608 | tf_op jit(solution)/shard_map/all_to_all | solution.py:258
  (388 shorter events, 204.7 us)
Async XLA Ops:
  7.2 10.8 %copy-start.6 = (bf16[512,1024]{1,0:T(8,128)(2,1)S(1)}, bf16[512,1024]{1,0:T(8,128)(2,1)}, u32[]{:S(2)}) copy-start(bf16[512,1024]{1,0:T(8,128)(2,1)} %param.14) | copy-start | bytes 3145732
  7.2 10.8 %copy-start.7 = (bf16[512,1024]{1,0:T(8,128)(2,1)S(1)}, bf16[512,1024]{1,0:T(8,128)(2,1)}, u32[]{:S(2)}) copy-start(bf16[512,1024]{1,0:T(8,128)(2,1)} %param.15) | copy-start | bytes 3145732
  7.2 245.8 %all-gather.2.cloned.1.call-start = ((), (), s32[]{:S(2)}) async-start(), calls=%async_computation.5 | async-start | bytes 17301504 | tf_op jit(solution)/shard_map/all_gather | solution.py:171
  8.5 7.7 collective-permute-start
  10.4 7.5 collective-permute-start.1
  14.8 4.2 copy-start.17
  18.9 1.5 copy-start.2
  20.5 4.8 copy-start.15
  121.3 12.5 %copy-start.8 = (bf16[512,1024]{1,0:T(8,128)(2,1)S(1)}, bf16[512,1024]{1,0:T(8,128)(2,1)}, u32[]{:S(2)}) copy-start(bf16[512,1024]{1,0:T(8,128)(2,1)} %param.13) | copy-start | bytes 3145732
  121.3 111.7 %all-to-all-start = ((bf16[2,256,64,128]{3,2,0,1:T(8,128)(2,1)}), bf16[2,256,64,128]{3,2,0,1:T(8,128)(2,1)}, u32[]{:S(2)}, u32[]{:S(2)}) async-start(bf16[2,256,64,128]{3,2,0,1:T(8,128)(2,1)} %bitcast.306), calls=%async_computation | async-start | bytes 16777216 | tf_op jit(solution)/shard_map/all_to_all | solution.py:209
  133.8 1.6 copy-start.9
  135.4 1.6 copy-start.10
  137.0 2.1 copy-start.3
  252.9 10.0 %copy-start.11 = (bf16[8,8,64,128]{3,2,1,0:T(8,128)(2,1)S(1)}, bf16[8,8,64,128]{3,2,1,0:T(8,128)(2,1)}, u32[]{:S(2)}) copy-start(bf16[8,8,64,128]{3,2,1,0:T(8,128)(2,1)} %custom-call.8) | copy-start | bytes 3145732
  402.8 3.8 copy-start.12
  454.9 11.5 %copy-start = (f32[8,10,64,128]{3,2,0,1:T(8,128)S(1)}, f32[8,10,64,128]{3,2,0,1:T(8,128)}, u32[]{:S(2)}) copy-start(f32[8,10,64,128]{3,2,0,1:T(8,128)} %get-tuple-element.256) | copy-start | bytes 7864324
  454.9 193.2 %all-to-all-start.2 = ((bf16[2,256,64,128]{3,2,0,1:T(8,128)(2,1)}), bf16[2,256,64,128]{3,2,0,1:T(8,128)(2,1)}, u32[]{:S(2)}, u32[]{:S(2)}) async-start(bf16[2,256,64,128]{3,2,0,1:T(8,128)(2,1)} %copy.144), calls=%async_computation.2 | async-start | bytes 16777216 | tf_op jit(solution)/shard_map/all_to_all | solution.py:237
  466.3 4.0 copy-start.13
  466.3 176.1 %all-reduce.9.cloned.1.call-start = ((), (), s32[]{:S(2)}) async-start(), calls=%async_computation.6 | async-start | bytes 2097152 | tf_op jit(solution)/shard_map/psum | solution.py:247
  466.4 3.9 copy-start.14
  468.2 102.2 %collective-permute-start.2 = (f32[2,8,64,128]{3,2,1,0:T(8,128)}, f32[2,8,64,128]{3,2,1,0:T(8,128)}, u32[]{:S(2)}, u32[]{:S(2)}) collective-permute-start(f32[2,8,64,128]{3,2,1,0:T(8,128)} %fusion.31), channel_id=1, source_target_pairs={{0,4},{4,8},{8,12},{12,16},{16,20},{20,24},{24,28},{28,32},{32,36}... | collective-permute-start | bytes 1572872 | tf_op jit(solution)/shard_map/ppermute | solution.py:19
  471.4 99.1 %copy-start.1 = (f32[8,10,64,128]{3,2,0,1:T(8,128)S(1)}, f32[8,10,64,128]{3,2,0,1:T(8,128)}, u32[]{:S(2)}) copy-start(f32[8,10,64,128]{3,2,0,1:T(8,128)} %get-tuple-element.255) | copy-start | bytes 7864324
  571.6 2.0 copy-start.4
  573.6 73.6 %collective-permute-start.3 = (f32[2,8,64,128]{3,2,1,0:T(8,128)S(1)}, f32[2,8,64,128]{3,2,1,0:T(8,128)S(1)}, u32[]{:S(2)}, u32[]{:S(2)}) collective-permute-start(f32[2,8,64,128]{3,2,1,0:T(8,128)S(1)} %get-tuple-element.375), channel_id=1, source_target_pairs={{4,0},{8,4},{12,8},{16,12},{20,16},{24,20},{28,24},{32,28},{36,32}... | collective-permute-start | bytes 1572872 | tf_op jit(solution)/shard_map/ppermute | solution.py:21
  598.7 45.3 %copy-start.16 = (f32[257]{0:T(512)}, f32[257]{0:T(512)S(1)}, u32[]{:S(2)}) copy-start(f32[257]{0:T(512)S(1)} %scatter_custom_fusion.3) | copy-start | bytes 3088
  642.4 2.5 copy-start.5
  647.2 5.2 slice-start
  648.1 84.6 %all-to-all-start.1 = ((bf16[4,128,1024]{2,1,0:T(8,128)(2,1)}), bf16[4,128,1024]{2,1,0:T(8,128)(2,1)S(1)}, u32[]{:S(2)}, u32[]{:S(2)}) async-start(bf16[4,128,1024]{2,1,0:T(8,128)(2,1)} %all_to_all.49), calls=%async_computation.1 | async-start | bytes 2097152 | tf_op jit(solution)/shard_map/all_to_all | solution.py:256
  716.9 6.8 copy-start.18
  732.7 19.6 %all-to-all-start.3 = ((bf16[4,128,1024]{2,1,0:T(8,128)(2,1)}), bf16[4,128,1024]{2,1,0:T(8,128)(2,1)S(1)}, u32[]{:S(2)}, u32[]{:S(2)}) async-start(bf16[4,128,1024]{2,1,0:T(8,128)(2,1)} %all_to_all.54), calls=%async_computation.3 | async-start | bytes 2097152 | tf_op jit(solution)/shard_map/all_to_all | solution.py:257
  752.3 17.2 %all-to-all-start.4 = ((bf16[4,128,1024]{2,1,0:T(8,128)(2,1)}), bf16[4,128,1024]{2,1,0:T(8,128)(2,1)S(1)}, u32[]{:S(2)}, u32[]{:S(2)}) async-start(bf16[4,128,1024]{2,1,0:T(8,128)(2,1)} %all_to_all.58), calls=%async_computation.4 | async-start | bytes 2097152 | tf_op jit(solution)/shard_map/all_to_all | solution.py:258
Sparse Core Ops, SparseCore 0:
  25.4 78.1 all-gather.1
  471.5 170.8 all-reduce.8
